TPU v7x, 128 devices: a whole 4x4x4 slice. The times are simulated.
128 devices in a mesh: section: 4 (over x), dp: 32 (over y, z, core).
Axes of the slice: x: 4, y: 4, z: 4, core: 2. Of those that a mesh axis runs over, the one named last changes fastest.
Arguments:
- tokens: bfloat16 [4096, 8192], P('dp'), may hold values from -6 to 6
- cotangent: bfloat16 [4096, 8192], P('dp'), may hold values from -6 to 6
- gains: float32 [4, 8192], P('section'), may hold values from 0.5 to 1.5
- value_projection_weight: bfloat16 [4, 8192, 1024], P('section', 'dp'), may hold values from -0.0625 to 0.0625
- output_projection_weight: bfloat16 [4, 8192, 1024], P('section', 'dp'), may hold values from -0.1875 to 0.1875
- block_adapter_ids: int32 [32], replicated, may hold values from 0 to 63
- job_adapter: int32 [32, 64], replicated, may hold values from -1 to 63, as said below
- job_slab: int32 [32, 64], replicated, may hold values from -1 to 15, as said below
- token_counts: int32 [64], replicated, may hold values from 128 to 1023
- slot_adapter_params: bfloat16 [4, 2048, 9216], P('section', 'dp'), may hold values from -0.29882812 to 0.29882812
- first_moment: float32 [4, 2048, 9216], P('section', 'dp'), may hold values from -6 to 6
- second_moment: float32 [4, 2048, 9216], P('section', 'dp'), may hold values from 0.1 to 10
Outputs:
- new_params: bfloat16 [4, 2048, 9216], P('section', 'dp')
- new_first: float32 [4, 2048, 9216], P('section', 'dp')
- new_second: float32 [4, 2048, 9216], P('section', 'dp')
- user_panels: bfloat16 [4, 32, 147456], P('section', 'dp')
Inputs may be any that keep to these rules, and one draw needn't show every extreme that they name: `job_adapter`: row o lists the adapters of which owner o holds a slab, each once, followed by -1; the 16 slabs of every adapter are held by 16 different owners, and every slab of every adapter is held exactly once. `job_slab`: the slab held in the same entry of job_adapter; -1 exactly where job_adapter is -1.
All inputs are finite; a program needn't handle non-finite values.
Results may differ from a plain program's by a relative error of at most 0.001.
Values may be sent and summed in bfloat16 or wider, within the bound.
No kernel may reach another device: no remote copies, remote signals or barrier semaphores. Data moves between devices by JAX's collectives and lax.ppermute only.
A program may use at most 128 MiB of HBM per device.

v0:
```python
import jax
import jax.numpy as jnp
from jax import lax
from jax.sharding import PartitionSpec as P

ADAPTER_RANK = 16
MROWS = 16


ADAPTER_SCALE = 2.0
LEARN_RATE = 0.001
BETA_FIRST = 0.9
BETA_SECOND = 0.999
ADAM_EPS = 1e-08
FIRST_FIX = 1.0 - 0.9**50 * 0.9**50
SECOND_FIX = 1.0 - 0.999**50 * 0.999**50
NORM_EPS = 1e-05


def from_behind(shard, axis, by):
    length = lax.axis_size(axis)
    pairs = [(i, i + by) for i in range(length) if 0 <= i + by < length]
    return lax.ppermute(shard, axis, pairs)


def contract_trailing(left, right):
    return lax.dot_general(
        left, right, (((1,), (1,)), ((), ())), preferred_element_type=jnp.float32
    )


def contract_leading(left, right):
    return lax.dot_general(
        left, right, (((0,), (0,)), ((), ())), preferred_element_type=jnp.float32
    )


def norm_rows(hidden_state, gain_vector_row):
    hidden_wide = hidden_state.astype(jnp.float32)
    mean_square = jnp.mean(hidden_wide * hidden_wide, axis=-1, keepdims=True)
    norm_gain_scale = lax.rsqrt(mean_square + NORM_EPS)
    normalized_rows = (hidden_wide * norm_gain_scale * gain_vector_row).astype(jnp.bfloat16)
    return (hidden_wide, norm_gain_scale, normalized_rows)


def layer_ahead_pass(
    hidden_state, gain_vector_row, value_complete, output_complete, adapter_down, adapter_up
):
    hidden_wide, norm_gain_scale, normalized_rows = norm_rows(hidden_state, gain_vector_row)
    rank_projected = jnp.dot(
        normalized_rows, adapter_down, preferred_element_type=jnp.float32
    ).astype(jnp.bfloat16)
    value_block_rows = (
        jnp.dot(normalized_rows, value_complete, preferred_element_type=jnp.float32)
        + ADAPTER_SCALE * jnp.dot(rank_projected, adapter_up, preferred_element_type=jnp.float32)
    ).astype(jnp.bfloat16)
    output_block_rows = (hidden_wide + contract_trailing(value_block_rows, output_complete)).astype(
        jnp.bfloat16
    )
    return (output_block_rows, norm_gain_scale, normalized_rows, rank_projected)


def layer_reverse_pass(
    output_gradient,
    hidden_state,
    norm_gain_scale,
    normalized_rows,
    rank_projected,
    gain_vector_row,
    value_complete,
    output_complete,
    adapter_down,
    adapter_up,
):
    value_gradient = jnp.dot(
        output_gradient, output_complete, preferred_element_type=jnp.float32
    ).astype(jnp.bfloat16)
    low_rank_gradient = (ADAPTER_SCALE * contract_trailing(value_gradient, adapter_up)).astype(
        jnp.bfloat16
    )
    down_gradient = contract_leading(normalized_rows, low_rank_gradient)
    up_gradient = ADAPTER_SCALE * contract_leading(rank_projected, value_gradient)
    normed_gradient = (
        contract_trailing(value_gradient, value_complete)
        + contract_trailing(low_rank_gradient, adapter_down)
    ) * gain_vector_row
    hidden_wide = hidden_state.astype(jnp.float32)
    centred = jnp.mean(hidden_wide * normed_gradient, axis=-1, keepdims=True)
    grad_in = (
        output_gradient.astype(jnp.float32)
        + norm_gain_scale * normed_gradient
        - hidden_wide * norm_gain_scale**3 * centred
    )
    return (grad_in.astype(jnp.bfloat16), down_gradient, up_gradient)


def adam_update(params_old, first_old, second_old, slot_grad, live):
    first_step = BETA_FIRST * first_old + (1.0 - BETA_FIRST) * slot_grad
    second_step = BETA_SECOND * second_old + (1.0 - BETA_SECOND) * slot_grad * slot_grad
    step_size = first_step / FIRST_FIX / (jnp.sqrt(second_step / SECOND_FIX) + ADAM_EPS)
    params_step = (params_old.astype(jnp.float32) - LEARN_RATE * step_size).astype(jnp.bfloat16)
    return (
        jnp.where(live, params_step, params_old),
        jnp.where(live, first_step, first_old),
        jnp.where(live, second_step, second_old),
    )


def put_slot(saved_array, new_value, slot_number, is_valid):
    current = lax.dynamic_index_in_dim(saved_array, slot_number, 0, keepdims=False)
    return lax.dynamic_update_index_in_dim(
        saved_array, jnp.where(is_valid, new_value, current), slot_number, 0
    )


def select_slot(saved_array, slot_number):
    return lax.dynamic_index_in_dim(saved_array, slot_number, 0, keepdims=False)


def on_device(
    tokens,
    cotangent,
    gains,
    value_projection_weight,
    output_projection_weight,
    block_adapter_ids,
    job_adapter,
    job_slab,
    token_counts,
    slot_adapter_params,
    first_moment,
    second_moment,
):
    section_index = lax.axis_index("section")
    owner_index = lax.axis_index("dp")
    section_total = lax.axis_size("section")
    owner_total = lax.axis_size("dp")
    tok_dev, hidden_width = tokens.shape
    value_feature_width = value_projection_weight.shape[2]
    panel_width = slot_adapter_params.shape[2]
    slab_count = owner_total // 2
    block_total = block_adapter_ids.shape[0]
    local_blocks = block_total // owner_total
    block_rows = tok_dev // local_blocks
    adapter_total = token_counts.shape[0]
    divide_position = hidden_width * ADAPTER_RANK
    value_complete, output_complete = (
        lax.all_gather(value_projection_weight, "dp", axis=1, tiled=True),
        lax.all_gather(output_projection_weight, "dp", axis=1, tiled=True),
    )
    value_complete = value_complete[0]
    output_complete = output_complete[0]
    gain_vector_row = gains[0]
    my_jobs = lax.dynamic_index_in_dim(job_adapter, owner_index, 0, keepdims=False)
    my_blocks = lax.dynamic_slice_in_dim(
        block_adapter_ids, owner_index * local_blocks, local_blocks
    )
    slab_ids = jnp.arange(slab_count, dtype=jnp.int32)
    matching = (job_adapter[None, None] == my_blocks[:, None, None, None]) & (
        job_slab[None, None] == slab_ids[None, :, None, None]
    )
    owner_ids = jnp.arange(owner_total, dtype=jnp.int32)
    source_owner = jnp.sum(jnp.where(matching, owner_ids[None, None, :, None], 0), axis=(2, 3))
    own_select = (block_adapter_ids[:, None] == my_jobs[None, :]) & (my_jobs[None, :] >= 0)
    slot_rows = jnp.arange(local_blocks, dtype=jnp.int32)[:, None]

    def hand_out(owned):
        picked = jnp.dot(own_select.astype(jnp.bfloat16), owned, preferred_element_type=jnp.float32)
        return picked.astype(jnp.bfloat16).reshape(owner_total, local_blocks, panel_width)

    def assemble(arrived):
        gathered_slabs = arrived[source_owner, slot_rows]
        return gathered_slabs.reshape(local_blocks, slab_count * panel_width)

    gathered_panels = assemble(
        lax.all_to_all(
            hand_out(slot_adapter_params[0]), "dp", split_axis=0, concat_axis=0, tiled=True
        )
    )
    adapter_down_every = gathered_panels[:, :divide_position].reshape(
        local_blocks, hidden_width, ADAPTER_RANK
    )
    adapter_up_every = gathered_panels[:, divide_position:].reshape(
        local_blocks, ADAPTER_RANK, value_feature_width
    )
    micro_rows = MROWS
    micro_count = tok_dev // micro_rows
    per_block = block_rows // micro_rows
    step_count = section_total + micro_count - 1
    token_micro = tokens.reshape(micro_count, micro_rows, hidden_width)
    cot_micro = cotangent.reshape(micro_count, micro_rows, hidden_width)

    def forward_step(state_tuple, step_number):
        incoming, saved_in, saved_scale, saved_normed, saved_low = state_tuple
        micro_index = step_number - section_index
        is_valid = (micro_index >= 0) & (micro_index < micro_count)
        micro_slot = jnp.clip(micro_index, 0, micro_count - 1)
        hidden_state = jnp.where(section_index == 0, select_slot(token_micro, micro_slot), incoming)
        block_slot_index = micro_slot // per_block

        def forward_run_layer(unused):
            return layer_ahead_pass(
                hidden_state,
                gain_vector_row,
                value_complete,
                output_complete,
                select_slot(adapter_down_every, block_slot_index),
                select_slot(adapter_up_every, block_slot_index),
            )

        def forward_skip_layer(unused):
            return (
                jnp.zeros((micro_rows, hidden_width), jnp.bfloat16),
                jnp.zeros((micro_rows, 1), jnp.float32),
                jnp.zeros((micro_rows, hidden_width), jnp.bfloat16),
                jnp.zeros((micro_rows, ADAPTER_RANK), jnp.bfloat16),
            )

        output_block_rows, norm_gain_scale, normalized_rows, rank_projected = lax.cond(
            is_valid, forward_run_layer, forward_skip_layer, None
        )
        saved_in = put_slot(saved_in, hidden_state, micro_slot, is_valid)
        saved_scale = put_slot(saved_scale, norm_gain_scale, micro_slot, is_valid)
        saved_normed = put_slot(saved_normed, normalized_rows, micro_slot, is_valid)
        saved_low = put_slot(saved_low, rank_projected, micro_slot, is_valid)
        passed = from_behind(output_block_rows, "section", 1)
        return ((passed, saved_in, saved_scale, saved_normed, saved_low), None)

    forward_init = (
        jnp.zeros((micro_rows, hidden_width), jnp.bfloat16),
        jnp.zeros((micro_count, micro_rows, hidden_width), jnp.bfloat16),
        jnp.zeros((micro_count, micro_rows, 1), jnp.float32),
        jnp.zeros((micro_count, micro_rows, hidden_width), jnp.bfloat16),
        jnp.zeros((micro_count, micro_rows, ADAPTER_RANK), jnp.bfloat16),
    )
    forward_done, _ = lax.scan(forward_step, forward_init, jnp.arange(step_count, dtype=jnp.int32))
    _, saved_in, saved_scale, saved_normed, saved_low = forward_done

    def backward_step(state_tuple, step_number):
        incoming, block_grads = state_tuple
        micro_index = step_number - (section_total - 1 - section_index)
        is_valid = (micro_index >= 0) & (micro_index < micro_count)
        micro_slot = jnp.clip(micro_index, 0, micro_count - 1)
        output_gradient = jnp.where(
            section_index == section_total - 1, select_slot(cot_micro, micro_slot), incoming
        )
        block_slot_index = micro_slot // per_block

        def backward_run_layer(unused):
            return layer_reverse_pass(
                output_gradient,
                select_slot(saved_in, micro_slot),
                select_slot(saved_scale, micro_slot),
                select_slot(saved_normed, micro_slot),
                select_slot(saved_low, micro_slot),
                gain_vector_row,
                value_complete,
                output_complete,
                select_slot(adapter_down_every, block_slot_index),
                select_slot(adapter_up_every, block_slot_index),
            )

        def backward_skip_layer(unused):
            return (
                jnp.zeros((micro_rows, hidden_width), jnp.bfloat16),
                jnp.zeros((hidden_width, ADAPTER_RANK), jnp.float32),
                jnp.zeros((ADAPTER_RANK, value_feature_width), jnp.float32),
            )

        grad_in, down_gradient, up_gradient = lax.cond(
            is_valid, backward_run_layer, backward_skip_layer, None
        )
        grad_term = jnp.concatenate([down_gradient.reshape(-1), up_gradient.reshape(-1)])
        block_grads = block_grads.at[block_slot_index].add(jnp.where(is_valid, grad_term, 0.0))
        passed = from_behind(grad_in, "section", -1)
        return ((passed, block_grads), None)

    backward_init = (
        jnp.zeros((micro_rows, hidden_width), jnp.bfloat16),
        jnp.zeros((local_blocks, slab_count * panel_width), jnp.float32),
    )
    backward_done, _ = lax.scan(
        backward_step, backward_init, jnp.arange(step_count, dtype=jnp.int32)
    )
    block_grads = backward_done[1]
    outgoing = (
        jnp.zeros((owner_total, local_blocks, panel_width), jnp.float32)
        .at[source_owner, slot_rows]
        .set(block_grads.reshape(local_blocks, slab_count, panel_width))
    )
    arrived = lax.all_to_all(
        outgoing.astype(jnp.bfloat16), "dp", split_axis=0, concat_axis=0, tiled=True
    ).astype(outgoing.dtype)
    summed = jnp.dot(
        own_select.astype(jnp.float32).T,
        arrived.reshape(block_total, panel_width),
        precision=lax.Precision.HIGHEST,
        preferred_element_type=jnp.float32,
    )
    live = my_jobs >= 0
    adapter_ids = jnp.arange(adapter_total, dtype=jnp.int32)
    slot_counts = jnp.sum(
        jnp.where(adapter_ids[None, :] == my_jobs[:, None], token_counts[None, :], 0), axis=1
    )
    slot_counts = jnp.where(live, slot_counts, 1)
    slot_grad = summed / slot_counts.astype(jnp.float32)[:, None]
    params_new, first_new, second_new = adam_update(
        slot_adapter_params[0], first_moment[0], second_moment[0], slot_grad, live[:, None]
    )
    returned = assemble(
        lax.all_to_all(hand_out(params_new), "dp", split_axis=0, concat_axis=0, tiled=True)
    )
    return (params_new[None], first_new[None], second_new[None], returned[None])


def solution(mesh):
    return jax.shard_map(
        on_device,
        mesh=mesh,
        in_specs=(
            P("dp", None),
            P("dp", None),
            P("section", None),
            P("section", "dp", None),
            P("section", "dp", None),
            P(),
            P(),
            P(),
            P(),
            P("section", "dp", None),
            P("section", "dp", None),
            P("section", "dp", None),
        ),
        out_specs=(
            P("section", "dp", None),
            P("section", "dp", None),
            P("section", "dp", None),
            P("section", "dp", None),
        ),
        check_vma=False,
    )
```

profile of v0, /device:TPU:1, one launch (start us, length us, event | category | flops | bytes accessed | tf_op | source)
XLA Modules:
  0.0 1005.0 jit_solution(1554221455761827771)
XLA Ops:
  48.8 42.7 %all-gather.3.cloned.1.call-done = bf16[1,8192,1024]{2,1,0:T(8,128)(2,1)} async-done(((bf16[1,256,1024]{2,1,0:T(8,128)(2,1)}), bf16[1,8192,1024]{2,1,0:T(8,128)(2,1)}) %all-gather.3.cloned.1.call-update) | async-done | bytes 16777232 | tf_op jit(solution)/shard_map/all_gather | solution.py:148
  91.6 74.4 %all-gather.5.cloned.1.call-done = bf16[1,8192,1024]{2,1,0:T(8,128)(2,1)} async-done(((bf16[1,256,1024]{2,1,0:T(8,128)(2,1)}), bf16[1,8192,1024]{2,1,0:T(8,128)(2,1)}) %all-gather.5.cloned.1.call-update) | async-done | bytes 16777232 | tf_op jit(solution)/shard_map/all_gather | solution.py:149
  169.0 320.4 %while.36 = (s32[]{:T(128)}, bf16[16,8192]{1,0:T(8,128)(2,1)S(1)}, bf16[8,16,8192]{2,1,0:T(8,128)(2,1)}, f32[8,16,1]{1,2,0:T(1,128)S(1)}, bf16[8,16,8192]{2,1,0:...) while((s32[]{:T(128)}, bf16[16,8192]{1,0:T(8,128)(2,1)S(1)}, ...), condition=%wide.region_5.6_spmd, body=%wide.region_1.5_spmd.sunk | while | flops 543343104 | bytes 42153352 | solution.py:236
  173.0 19.6 %conditional.5 = (bf16[16,8192]{1,0:T(8,128)(2,1)S(1)}, f32[16,1]{0,1:T(1,128)S(1)}, bf16[16,8192]{1,0:T(8,128)(2,1)S(1)}, bf16[16,16]{1,0:T(8,128)(2,1)}) conditional(s32[]{:T(128)} %convert_element_type.134, () %tuple.117, (bf16[16,8192]{1,0:T(8,128)(2,1)S(1)}, f32[1,8192]{1,0:T(1,128)S(1)}, bf16[8192,1024]{1,0:T(8,128)(2,1)}, ...), branch_computations={%region_2.2_spmd, %region_3.4_spmd} | conditional | flops 542949632 | bytes 37946776 | solution.py:219
  203.6 19.6 %conditional.5 = (bf16[16,8192]{1,0:T(8,128)(2,1)S(1)}, f32[16,1]{0,1:T(1,128)S(1)}, bf16[16,8192]{1,0:T(8,128)(2,1)S(1)}, bf16[16,16]{1,0:T(8,128)(2,1)}) conditional(s32[]{:T(128)} %convert_element_type.134, () %tuple.117, (bf16[16,8192]{1,0:T(8,128)(2,1)S(1)}, f32[1,8192]{1,0:T(1,128)S(1)}, bf16[8192,1024]{1,0:T(8,128)(2,1)}, ...), branch_computations={%region_2.2_spmd, %region_3.4_spmd} | conditional | flops 542949632 | bytes 37946776 | solution.py:219
  236.0 19.6 %conditional.5 = (bf16[16,8192]{1,0:T(8,128)(2,1)S(1)}, f32[16,1]{0,1:T(1,128)S(1)}, bf16[16,8192]{1,0:T(8,128)(2,1)S(1)}, bf16[16,16]{1,0:T(8,128)(2,1)}) conditional(s32[]{:T(128)} %convert_element_type.134, () %tuple.117, (bf16[16,8192]{1,0:T(8,128)(2,1)S(1)}, f32[1,8192]{1,0:T(1,128)S(1)}, bf16[8192,1024]{1,0:T(8,128)(2,1)}, ...), branch_computations={%region_2.2_spmd, %region_3.4_spmd} | conditional | flops 542949632 | bytes 37946776 | solution.py:219
  267.7 19.6 %conditional.5 = (bf16[16,8192]{1,0:T(8,128)(2,1)S(1)}, f32[16,1]{0,1:T(1,128)S(1)}, bf16[16,8192]{1,0:T(8,128)(2,1)S(1)}, bf16[16,16]{1,0:T(8,128)(2,1)}) conditional(s32[]{:T(128)} %convert_element_type.134, () %tuple.117, (bf16[16,8192]{1,0:T(8,128)(2,1)S(1)}, f32[1,8192]{1,0:T(1,128)S(1)}, bf16[8192,1024]{1,0:T(8,128)(2,1)}, ...), branch_computations={%region_2.2_spmd, %region_3.4_spmd} | conditional | flops 542949632 | bytes 37946776 | solution.py:219
  329.3 19.6 %conditional.5 = (bf16[16,8192]{1,0:T(8,128)(2,1)S(1)}, f32[16,1]{0,1:T(1,128)S(1)}, bf16[16,8192]{1,0:T(8,128)(2,1)S(1)}, bf16[16,16]{1,0:T(8,128)(2,1)}) conditional(s32[]{:T(128)} %convert_element_type.134, () %tuple.117, (bf16[16,8192]{1,0:T(8,128)(2,1)S(1)}, f32[1,8192]{1,0:T(1,128)S(1)}, bf16[8192,1024]{1,0:T(8,128)(2,1)}, ...), branch_computations={%region_2.2_spmd, %region_3.4_spmd} | conditional | flops 542949632 | bytes 37946776 | solution.py:219
  360.0 19.6 %conditional.5 = (bf16[16,8192]{1,0:T(8,128)(2,1)S(1)}, f32[16,1]{0,1:T(1,128)S(1)}, bf16[16,8192]{1,0:T(8,128)(2,1)S(1)}, bf16[16,16]{1,0:T(8,128)(2,1)}) conditional(s32[]{:T(128)} %convert_element_type.134, () %tuple.117, (bf16[16,8192]{1,0:T(8,128)(2,1)S(1)}, f32[1,8192]{1,0:T(1,128)S(1)}, bf16[8192,1024]{1,0:T(8,128)(2,1)}, ...), branch_computations={%region_2.2_spmd, %region_3.4_spmd} | conditional | flops 542949632 | bytes 37946776 | solution.py:219
  390.7 19.6 %conditional.5 = (bf16[16,8192]{1,0:T(8,128)(2,1)S(1)}, f32[16,1]{0,1:T(1,128)S(1)}, bf16[16,8192]{1,0:T(8,128)(2,1)S(1)}, bf16[16,16]{1,0:T(8,128)(2,1)}) conditional(s32[]{:T(128)} %convert_element_type.134, () %tuple.117, (bf16[16,8192]{1,0:T(8,128)(2,1)S(1)}, f32[1,8192]{1,0:T(1,128)S(1)}, bf16[8192,1024]{1,0:T(8,128)(2,1)}, ...), branch_computations={%region_2.2_spmd, %region_3.4_spmd} | conditional | flops 542949632 | bytes 37946776 | solution.py:219
  422.0 22.7 %collective-permute-start = (bf16[16,8192]{1,0:T(8,128)(2,1)S(1)}, bf16[16,8192]{1,0:T(8,128)(2,1)S(1)}, u32[]{:S(2)}, u32[]{:S(2)}) collective-permute-start(bf16[16,8192]{1,0:T(8,128)(2,1)S(1)} %get-tuple-element.992), channel_id=1, source_target_pairs={{0,32},{32,64},{64,96},{1,33},{33,65},{65,97},{2,34},{34,66},{66,9... | collective-permute-start | bytes 786440 | tf_op jit(solution)/shard_map/while/body/eval_jaxpr/ppermute | solution.py:23
  464.4 21.8 %collective-permute-start = (bf16[16,8192]{1,0:T(8,128)(2,1)S(1)}, bf16[16,8192]{1,0:T(8,128)(2,1)S(1)}, u32[]{:S(2)}, u32[]{:S(2)}) collective-permute-start(bf16[16,8192]{1,0:T(8,128)(2,1)S(1)} %get-tuple-element.992), channel_id=1, source_target_pairs={{0,32},{32,64},{64,96},{1,33},{33,65},{65,97},{2,34},{34,66},{66,9... | collective-permute-start | bytes 786440 | tf_op jit(solution)/shard_map/while/body/eval_jaxpr/ppermute | solution.py:23
  489.5 427.2 %while.37 = (s32[]{:T(128)}, bf16[16,8192]{1,0:T(8,128)(2,1)S(1)}, f32[1,147456]{1,0:T(1,128)S(1)}, s32[11]{0:T(128)S(1)}, s32[]{:T(128)}, /*index=5*/pred[]{:T(...) while((s32[]{:T(128)}, bf16[16,8192]{1,0:T(8,128)(2,1)S(1)}, ...), condition=%wide.region_11.12_spmd.clone, body=%wide.region_6.11_spmd.clone.sunk | while | flops 549044800 | bytes 42802872 | solution.py:282
  506.2 19.6 %collective-permute-done.1 = bf16[16,8192]{1,0:T(8,128)(2,1)S(1)} collective-permute-done((bf16[16,8192]{1,0:T(8,128)(2,1)S(1)}, bf16[16,8192]{1,0:T(8,128)(2,1)S(1)}, u32[]{:S(2)}, u32[]{:S(2)}) %collective-permute-start.1) | collective-permute-done | bytes 262176 | tf_op jit(solution)/shard_map/while/body/eval_jaxpr/ppermute | solution.py:23
  532.6 87.0 %collective-permute-done.1 = bf16[16,8192]{1,0:T(8,128)(2,1)S(1)} collective-permute-done((bf16[16,8192]{1,0:T(8,128)(2,1)S(1)}, bf16[16,8192]{1,0:T(8,128)(2,1)S(1)}, u32[]{:S(2)}, u32[]{:S(2)}) %collective-permute-start.1) | collective-permute-done | bytes 262176 | tf_op jit(solution)/shard_map/while/body/eval_jaxpr/ppermute | solution.py:23
  620.9 28.8 %conditional.6 = (bf16[16,8192]{1,0:T(8,128)(2,1)S(1)}, f32[1,131072]{1,0:T(1,128)S(1)}, f32[1,16384]{1,0:T(1,128)S(1)}) conditional(s32[]{:T(128)} %convert_element_type.135, () %tuple.120, (pred[]{:T(512)}, bf16[8,16,8192]{2,1,0:T(8,128)(2,1)}, s32[]{:T(128)}, bf16[16,8192]{1,0:T(8,128)(2,1)S(1)}, f32[8,16,1]{1,2,0:T(1,128)S(1)}, ...), branch_computations={%region_7.7_spmd, %region_8.9_spmd} | conditional | flops 548307520 | bytes 39984272 | solution.py:270
  658.0 28.8 %conditional.6 = (bf16[16,8192]{1,0:T(8,128)(2,1)S(1)}, f32[1,131072]{1,0:T(1,128)S(1)}, f32[1,16384]{1,0:T(1,128)S(1)}) conditional(s32[]{:T(128)} %convert_element_type.135, () %tuple.120, (pred[]{:T(512)}, bf16[8,16,8192]{2,1,0:T(8,128)(2,1)}, s32[]{:T(128)}, bf16[16,8192]{1,0:T(8,128)(2,1)S(1)}, f32[8,16,1]{1,2,0:T(1,128)S(1)}, ...), branch_computations={%region_7.7_spmd, %region_8.9_spmd} | conditional | flops 548307520 | bytes 39984272 | solution.py:270
  695.1 28.8 %conditional.6 = (bf16[16,8192]{1,0:T(8,128)(2,1)S(1)}, f32[1,131072]{1,0:T(1,128)S(1)}, f32[1,16384]{1,0:T(1,128)S(1)}) conditional(s32[]{:T(128)} %convert_element_type.135, () %tuple.120, (pred[]{:T(512)}, bf16[8,16,8192]{2,1,0:T(8,128)(2,1)}, s32[]{:T(128)}, bf16[16,8192]{1,0:T(8,128)(2,1)S(1)}, f32[8,16,1]{1,2,0:T(1,128)S(1)}, ...), branch_computations={%region_7.7_spmd, %region_8.9_spmd} | conditional | flops 548307520 | bytes 39984272 | solution.py:270
  732.3 28.8 %conditional.6 = (bf16[16,8192]{1,0:T(8,128)(2,1)S(1)}, f32[1,131072]{1,0:T(1,128)S(1)}, f32[1,16384]{1,0:T(1,128)S(1)}) conditional(s32[]{:T(128)} %convert_element_type.135, () %tuple.120, (pred[]{:T(512)}, bf16[8,16,8192]{2,1,0:T(8,128)(2,1)}, s32[]{:T(128)}, bf16[16,8192]{1,0:T(8,128)(2,1)S(1)}, f32[8,16,1]{1,2,0:T(1,128)S(1)}, ...), branch_computations={%region_7.7_spmd, %region_8.9_spmd} | conditional | flops 548307520 | bytes 39984272 | solution.py:270
  769.4 28.8 %conditional.6 = (bf16[16,8192]{1,0:T(8,128)(2,1)S(1)}, f32[1,131072]{1,0:T(1,128)S(1)}, f32[1,16384]{1,0:T(1,128)S(1)}) conditional(s32[]{:T(128)} %convert_element_type.135, () %tuple.120, (pred[]{:T(512)}, bf16[8,16,8192]{2,1,0:T(8,128)(2,1)}, s32[]{:T(128)}, bf16[16,8192]{1,0:T(8,128)(2,1)S(1)}, f32[8,16,1]{1,2,0:T(1,128)S(1)}, ...), branch_computations={%region_7.7_spmd, %region_8.9_spmd} | conditional | flops 548307520 | bytes 39984272 | solution.py:270
  806.5 28.8 %conditional.6 = (bf16[16,8192]{1,0:T(8,128)(2,1)S(1)}, f32[1,131072]{1,0:T(1,128)S(1)}, f32[1,16384]{1,0:T(1,128)S(1)}) conditional(s32[]{:T(128)} %convert_element_type.135, () %tuple.120, (pred[]{:T(512)}, bf16[8,16,8192]{2,1,0:T(8,128)(2,1)}, s32[]{:T(128)}, bf16[16,8192]{1,0:T(8,128)(2,1)S(1)}, f32[8,16,1]{1,2,0:T(1,128)S(1)}, ...), branch_computations={%region_7.7_spmd, %region_8.9_spmd} | conditional | flops 548307520 | bytes 39984272 | solution.py:270
  843.7 28.8 %conditional.6 = (bf16[16,8192]{1,0:T(8,128)(2,1)S(1)}, f32[1,131072]{1,0:T(1,128)S(1)}, f32[1,16384]{1,0:T(1,128)S(1)}) conditional(s32[]{:T(128)} %convert_element_type.135, () %tuple.120, (pred[]{:T(512)}, bf16[8,16,8192]{2,1,0:T(8,128)(2,1)}, s32[]{:T(128)}, bf16[16,8192]{1,0:T(8,128)(2,1)S(1)}, f32[8,16,1]{1,2,0:T(1,128)S(1)}, ...), branch_computations={%region_7.7_spmd, %region_8.9_spmd} | conditional | flops 548307520 | bytes 39984272 | solution.py:270
  880.8 28.8 %conditional.6 = (bf16[16,8192]{1,0:T(8,128)(2,1)S(1)}, f32[1,131072]{1,0:T(1,128)S(1)}, f32[1,16384]{1,0:T(1,128)S(1)}) conditional(s32[]{:T(128)} %convert_element_type.135, () %tuple.120, (pred[]{:T(512)}, bf16[8,16,8192]{2,1,0:T(8,128)(2,1)}, s32[]{:T(128)}, bf16[16,8192]{1,0:T(8,128)(2,1)S(1)}, f32[8,16,1]{1,2,0:T(1,128)S(1)}, ...), branch_computations={%region_7.7_spmd, %region_8.9_spmd} | conditional | flops 548307520 | bytes 39984272 | solution.py:270
  926.8 28.0 %all-to-all-start.1 = ((bf16[32,2,4608]{2,1,0:T(2,128)(2,1)}), bf16[32,2,4608]{2,1,0:T(2,128)(2,1)S(1)}, u32[]{:S(2)}, u32[]{:S(2)}) async-start(bf16[32,2,4608]{2,1,0:T(2,128)(2,1)} %reshape.278), calls=%async_computation.1 | async-start | bytes 1179648 | tf_op jit(solution)/shard_map/all_to_all | solution.py:291
  (448 shorter events, 700.1 us)
Async XLA Ops:
  7.2 84.4 %all-gather.3.cloned.1.call-start = ((), (), s32[]{:S(2)}) async-start(), calls=%async_computation.3 | async-start | bytes 17301504 | tf_op jit(solution)/shard_map/all_gather | solution.py:148
  7.9 158.0 %all-gather.5.cloned.1.call-start = ((), (), s32[]{:S(2)}) async-start(), calls=%async_computation.4 | async-start | bytes 17301504 | tf_op jit(solution)/shard_map/all_gather | solution.py:149
  15.3 27.1 %all-to-all-start = ((bf16[32,2,4608]{2,1,0:T(2,128)(2,1)}), bf16[32,2,4608]{2,1,0:T(2,128)(2,1)S(1)}, u32[]{:S(2)}, u32[]{:S(2)}) async-start(bf16[32,2,4608]{2,1,0:T(2,128)(2,1)} %reshape.276), calls=%async_computation | async-start | bytes 1179648 | tf_op jit(solution)/shard_map/all_to_all | solution.py:176
  223.1 8.9 collective-permute-start
  255.6 8.1 collective-permute-start
  287.2 7.4 collective-permute-start
  318.2 7.1 collective-permute-start
  348.9 7.1 collective-permute-start
  410.2 7.1 collective-permute-start
  422.0 26.0 %collective-permute-start = (bf16[16,8192]{1,0:T(8,128)(2,1)S(1)}, bf16[16,8192]{1,0:T(8,128)(2,1)S(1)}, u32[]{:S(2)}, u32[]{:S(2)}) collective-permute-start(bf16[16,8192]{1,0:T(8,128)(2,1)S(1)} %get-tuple-element.992), channel_id=1, source_target_pairs={{0,32},{32,64},{64,96},{1,33},{33,65},{65,97},{2,34},{34,66},{66,9... | collective-permute-start | bytes 786440 | tf_op jit(solution)/shard_map/while/body/eval_jaxpr/ppermute | solution.py:23
  464.4 25.1 %collective-permute-start = (bf16[16,8192]{1,0:T(8,128)(2,1)S(1)}, bf16[16,8192]{1,0:T(8,128)(2,1)S(1)}, u32[]{:S(2)}, u32[]{:S(2)}) collective-permute-start(bf16[16,8192]{1,0:T(8,128)(2,1)S(1)} %get-tuple-element.992), channel_id=1, source_target_pairs={{0,32},{32,64},{64,96},{1,33},{33,65},{65,97},{2,34},{34,66},{66,9... | collective-permute-start | bytes 786440 | tf_op jit(solution)/shard_map/while/body/eval_jaxpr/ppermute | solution.py:23
  491.5 8.0 collective-permute-start.1
  501.1 24.8 %collective-permute-start.1 = (bf16[16,8192]{1,0:T(8,128)(2,1)S(1)}, bf16[16,8192]{1,0:T(8,128)(2,1)S(1)}, u32[]{:S(2)}, u32[]{:S(2)}) collective-permute-start(bf16[16,8192]{1,0:T(8,128)(2,1)S(1)} %get-tuple-element.1013), channel_id=1, source_target_pairs={{32,0},{64,32},{96,64},{33,1},{65,33},{97,65},{34,2},{66,34},{98,6... | collective-permute-start | bytes 786440 | tf_op jit(solution)/shard_map/while/body/eval_jaxpr/ppermute | solution.py:23
  527.5 92.2 %collective-permute-start.1 = (bf16[16,8192]{1,0:T(8,128)(2,1)S(1)}, bf16[16,8192]{1,0:T(8,128)(2,1)S(1)}, u32[]{:S(2)}, u32[]{:S(2)}) collective-permute-start(bf16[16,8192]{1,0:T(8,128)(2,1)S(1)} %get-tuple-element.1013), channel_id=1, source_target_pairs={{32,0},{64,32},{96,64},{33,1},{65,33},{97,65},{34,2},{66,34},{98,6... | collective-permute-start | bytes 786440 | tf_op jit(solution)/shard_map/while/body/eval_jaxpr/ppermute | solution.py:23
  649.6 7.1 collective-permute-start.1
  686.8 7.1 collective-permute-start.1
  723.9 7.1 collective-permute-start.1
  761.0 7.1 collective-permute-start.1
  798.2 7.1 collective-permute-start.1
  835.3 7.1 collective-permute-start.1
  872.5 7.1 collective-permute-start.1
  909.6 7.1 collective-permute-start.1
  926.8 40.3 %all-to-all-start.1 = ((bf16[32,2,4608]{2,1,0:T(2,128)(2,1)}), bf16[32,2,4608]{2,1,0:T(2,128)(2,1)S(1)}, u32[]{:S(2)}, u32[]{:S(2)}) async-start(bf16[32,2,4608]{2,1,0:T(2,128)(2,1)} %reshape.278), calls=%async_computation.1 | async-start | bytes 1179648 | tf_op jit(solution)/shard_map/all_to_all | solution.py:291
  978.9 15.9 %all-to-all-start.2 = ((bf16[32,2,4608]{2,1,0:T(2,128)(2,1)}), bf16[32,2,4608]{2,1,0:T(2,128)(2,1)S(1)}, u32[]{:S(2)}, u32[]{:S(2)}) async-start(bf16[32,2,4608]{2,1,0:T(2,128)(2,1)} %reshape.280), calls=%async_computation.2 | async-start | bytes 1179648 | tf_op jit(solution)/shard_map/all_to_all | solution.py:311
  (34 other events, 608.7 us)
Sparse Core Ops, SparseCore 0:
  10.2 81.2 all-gather.2
  93.8 72.0 all-gather.4
where the time goes:
time: 1020 us; the launch traced here: 1000 us
  matrix products  352 us (35%)
  waiting for transfers between devices  293 us (29%)
  starting transfers between devices  133 us (13%)
  other arithmetic  107 us (10%)
  local copies, waits for them, and re-layouts  89.5 us (9%)
  loops' own time  16.6 us (2%)
  between operations  14.6 us (1%)
    dot_general x32, matrix products, contract_trailing(): lax.dot_general(left, right, (((1,), (1,)), ((), ())), preferred_element_...  176 us
    ppermute x22, waiting for transfers between devices, from_behind(): return lax.ppermute(shard, axis, pairs)  141 us
    ppermute x22, starting transfers between devices, from_behind(): return lax.ppermute(shard, axis, pairs)  91.5 us
    all_gather x1, waiting for transfers between devices, on_device(): lax.all_gather(output_projection_weight, 'dp', axis=1, tiled=True)  74.4 us
    dot_general x8, matrix products, layer_reverse_pass(): jnp.dot(output_gradient, output_complete, preferred_element_type=jnp.floa...  65.1 us
    dot_general x8, matrix products, layer_ahead_pass(): jnp.dot(normalized_rows, value_complete, preferred_element_type=jnp.float32)  64.4 us
    all_gather x1, waiting for transfers between devices, on_device(): lax.all_gather(value_projection_weight, 'dp', axis=1, tiled=True)  42.7 us
    scatter-add x11, other arithmetic, backward_step(): block_grads.at[block_slot_index].add(jnp.where(is_valid, grad_term, 0.0))  33.9 us
  transfers between devices with their start and end apart: 27, of which 27 were waited for; matrix products, arithmetic and copies ran while one was open for 9% of the time, Pallas kernels for 0%

commit v1 on v0

v1 whole, which is shorter than its diff:
```python
import jax
import jax.numpy as jnp
from jax import lax
from jax.experimental import pallas as pl
from jax.experimental.pallas import tpu as pltpu
from jax.sharding import PartitionSpec as P

ADAPTER_RANK = 16
MICRO = 4
LAG = 2
CHUNK = 1024

ADAPTER_SCALE = 2.0
LEARN_RATE = 0.001
BETA_FIRST = 0.9
BETA_SECOND = 0.999
ADAM_EPS = 1e-08
FIRST_FIX = 1.0 - 0.9**50 * 0.9**50
SECOND_FIX = 1.0 - 0.999**50 * 0.999**50
NORM_EPS = 1e-05
F32 = jnp.float32
BF16 = jnp.bfloat16


def contract_trailing(left, right):
    return lax.dot_general(
        left, right, (((1,), (1,)), ((), ())), preferred_element_type=F32
    )


def contract_leading(left, right):
    return lax.dot_general(
        left, right, (((0,), (0,)), ((), ())), preferred_element_type=F32
    )


def plain_dot(left, right):
    return jnp.dot(left, right, preferred_element_type=F32)


def ahead_kernel(h_ref, down_ref, up_ref, value_ref, output_ref, next_ref, u_ref, low_ref, scale_ref, sum_ref, v_ref):
    step = pl.program_id(0)
    chunks = pl.num_programs(0) // 2
    width = h_ref.shape[1] * chunks

    @pl.when(step == 0)
    def _():
        u_ref[...] = jnp.zeros_like(u_ref)
        low_ref[...] = jnp.zeros_like(low_ref)
        sum_ref[...] = jnp.zeros_like(sum_ref)

    @pl.when(step < chunks)
    def _():
        rows = h_ref[...]
        wide = rows.astype(F32)
        u_ref[...] += plain_dot(rows, value_ref[...])
        low_ref[...] += contract_trailing(rows, down_ref[...])
        sum_ref[...] += jnp.sum(wide * wide, axis=-1, keepdims=True)

    @pl.when(step == chunks - 1)
    def _():
        scale = lax.rsqrt(sum_ref[...] / width + NORM_EPS)
        scale_ref[...] = scale
        low = (scale * low_ref[...]).astype(BF16)
        v_ref[...] = (
            scale * u_ref[...] + ADAPTER_SCALE * plain_dot(low, up_ref[...])
        ).astype(BF16)

    @pl.when(step >= chunks)
    def _():
        next_ref[...] = (
            h_ref[...].astype(F32) + contract_trailing(v_ref[...], output_ref[...])
        ).astype(BF16)


def ahead(hidden, down_t, up, value_full, output_full):
    rows, width = hidden.shape
    features = up.shape[1]
    chunks = width // CHUNK
    whole = lambda i: (0, 0)
    return pl.pallas_call(
        ahead_kernel,
        grid=(2 * chunks,),
        in_specs=[
            pl.BlockSpec((rows, CHUNK), lambda i: (0, i % chunks)),
            pl.BlockSpec((ADAPTER_RANK, CHUNK), lambda i: (0, jnp.minimum(i, chunks - 1))),
            pl.BlockSpec((ADAPTER_RANK, features), whole),
            pl.BlockSpec((CHUNK, features), lambda i: (jnp.minimum(i, chunks - 1), 0)),
            pl.BlockSpec((CHUNK, features), lambda i: (jnp.maximum(i - chunks, 0), 0)),
        ],
        out_specs=(
            pl.BlockSpec((rows, CHUNK), lambda i: (0, jnp.maximum(i - chunks, 0))),
            pl.BlockSpec((rows, features), whole),
            pl.BlockSpec((rows, ADAPTER_RANK), whole),
            pl.BlockSpec((rows, 1), whole),
        ),
        out_shape=(
            jax.ShapeDtypeStruct((rows, width), BF16),
            jax.ShapeDtypeStruct((rows, features), F32),
            jax.ShapeDtypeStruct((rows, ADAPTER_RANK), F32),
            jax.ShapeDtypeStruct((rows, 1), F32),
        ),
        scratch_shapes=[
            pltpu.VMEM((rows, 1), F32),
            pltpu.VMEM((rows, features), BF16),
        ],
        compiler_params=pltpu.CompilerParams(vmem_limit_bytes=24 * 2**20),
        name="ahead",
    )(hidden, down_t, up, value_full, output_full)


def reverse_kernel(
    grad_ref, output_ref, value_ref, down_ref, up_ref, h_ref, u_ref, low_ref, scale_ref,
    prev_ref, gv_ref, gl_ref, acc_ref, coef_ref,
):
    step = pl.program_id(0)
    chunks = pl.num_programs(0) // 2
    width = grad_ref.shape[1] * chunks

    @pl.when(step == 0)
    def _():
        acc_ref[...] = jnp.zeros_like(acc_ref)

    @pl.when(step < chunks)
    def _():
        acc_ref[...] += plain_dot(grad_ref[...], output_ref[...])

    @pl.when(step == chunks - 1)
    def _():
        gv = acc_ref[...].astype(BF16)
        gl = (ADAPTER_SCALE * contract_trailing(gv, up_ref[...])).astype(BF16)
        gv_ref[...] = gv
        gl_ref[...] = gl
        scale = scale_ref[...]
        centred = (
            jnp.sum(gv.astype(F32) * u_ref[...], axis=-1, keepdims=True)
            + jnp.sum(gl.astype(F32) * low_ref[...], axis=-1, keepdims=True)
        ) / width
        coef_ref[...] = scale * scale * scale * centred

    @pl.when(step >= chunks)
    def _():
        grad_norm = contract_trailing(gv_ref[...], value_ref[...]) + plain_dot(gl_ref[...], down_ref[...])
        prev_ref[...] = (
            grad_ref[...].astype(F32)
            + scale_ref[...] * grad_norm
            - h_ref[...].astype(F32) * coef_ref[...]
        ).astype(BF16)


def reverse(grad, output_full, value_full, down_t, up, hidden, u, low, scale):
    rows, width = grad.shape
    features = up.shape[1]
    chunks = width // CHUNK
    whole = lambda i: (0, 0)
    late = lambda i: (0, jnp.maximum(i - chunks, 0))
    return pl.pallas_call(
        reverse_kernel,
        grid=(2 * chunks,),
        in_specs=[
            pl.BlockSpec((rows, CHUNK), lambda i: (0, i % chunks)),
            pl.BlockSpec((CHUNK, features), lambda i: (jnp.minimum(i, chunks - 1), 0)),
            pl.BlockSpec((CHUNK, features), lambda i: (jnp.maximum(i - chunks, 0), 0)),
            pl.BlockSpec((ADAPTER_RANK, CHUNK), late),
            pl.BlockSpec((ADAPTER_RANK, features), whole),
            pl.BlockSpec((rows, CHUNK), late),
            pl.BlockSpec((rows, features), whole),
            pl.BlockSpec((rows, ADAPTER_RANK), whole),
            pl.BlockSpec((rows, 1), whole),
        ],
        out_specs=(
            pl.BlockSpec((rows, CHUNK), late),
            pl.BlockSpec((rows, features), whole),
            pl.BlockSpec((rows, ADAPTER_RANK), whole),
        ),
        out_shape=(
            jax.ShapeDtypeStruct((rows, width), BF16),
            jax.ShapeDtypeStruct((rows, features), BF16),
            jax.ShapeDtypeStruct((rows, ADAPTER_RANK), BF16),
        ),
        scratch_shapes=[pltpu.VMEM((rows, features), F32), pltpu.VMEM((rows, 1), F32)],
        compiler_params=pltpu.CompilerParams(vmem_limit_bytes=24 * 2**20),
        name="reverse",
    )(grad, output_full, value_full, down_t, up, hidden, u, low, scale)


def first_kernel(grad_ref, output_ref, up_ref, gv_ref, gl_ref, acc_ref):
    step = pl.program_id(0)

    @pl.when(step == 0)
    def _():
        acc_ref[...] = jnp.zeros_like(acc_ref)

    acc_ref[...] += plain_dot(grad_ref[...], output_ref[...])

    @pl.when(step == pl.num_programs(0) - 1)
    def _():
        gv = acc_ref[...].astype(BF16)
        gv_ref[...] = gv
        gl_ref[...] = (ADAPTER_SCALE * contract_trailing(gv, up_ref[...])).astype(BF16)


def reverse_first(grad, output_full, up):
    rows, width = grad.shape
    features = up.shape[1]
    whole = lambda i: (0, 0)
    return pl.pallas_call(
        first_kernel,
        grid=(width // CHUNK,),
        in_specs=[
            pl.BlockSpec((rows, CHUNK), lambda i: (0, i)),
            pl.BlockSpec((CHUNK, features), lambda i: (i, 0)),
            pl.BlockSpec((ADAPTER_RANK, features), whole),
        ],
        out_specs=(pl.BlockSpec((rows, features), whole), pl.BlockSpec((rows, ADAPTER_RANK), whole)),
        out_shape=(
            jax.ShapeDtypeStruct((rows, features), BF16),
            jax.ShapeDtypeStruct((rows, ADAPTER_RANK), BF16),
        ),
        scratch_shapes=[pltpu.VMEM((rows, features), F32)],
        compiler_params=pltpu.CompilerParams(vmem_limit_bytes=16 * 2**20),
        name="reverse_first",
    )(grad, output_full, up)


def spread_kernel(gv_ref, gl_ref, value_ref, down_ref, out_ref):
    out_ref[...] = contract_trailing(gv_ref[...], value_ref[...]) + plain_dot(gl_ref[...], down_ref[...])


def spread(gv, gl, value_full, down_t):
    rows, features = gv.shape
    width = value_full.shape[0]
    whole = lambda i: (0, 0)
    return pl.pallas_call(
        spread_kernel,
        grid=(width // CHUNK,),
        in_specs=[
            pl.BlockSpec((rows, features), whole),
            pl.BlockSpec((rows, ADAPTER_RANK), whole),
            pl.BlockSpec((CHUNK, features), lambda i: (i, 0)),
            pl.BlockSpec((ADAPTER_RANK, CHUNK), lambda i: (0, i)),
        ],
        out_specs=pl.BlockSpec((rows, CHUNK), lambda i: (0, i)),
        out_shape=jax.ShapeDtypeStruct((rows, width), F32),
        compiler_params=pltpu.CompilerParams(vmem_limit_bytes=16 * 2**20),
        name="spread",
    )(gv, gl, value_full, down_t)


def join_kernel(h_ref, norm_ref, grad_ref, down_ref, prev_ref, low_ref, scale_ref):
    width = h_ref.shape[1]
    rows = h_ref[...]
    wide = rows.astype(F32)
    grad_norm = norm_ref[...]
    low_ref[...] = contract_trailing(rows, down_ref[...])
    scale = lax.rsqrt(jnp.sum(wide * wide, axis=-1, keepdims=True) / width + NORM_EPS)
    scale_ref[...] = scale
    centred = jnp.sum(wide * grad_norm, axis=-1, keepdims=True) / width
    prev_ref[...] = (
        grad_ref[...].astype(F32) + scale * grad_norm - wide * (scale * scale * scale * centred)
    ).astype(BF16)


def join_last(hidden, grad_norm, grad, down_t):
    rows, width = hidden.shape
    return pl.pallas_call(
        join_kernel,
        out_shape=(
            jax.ShapeDtypeStruct((rows, width), BF16),
            jax.ShapeDtypeStruct((rows, ADAPTER_RANK), F32),
            jax.ShapeDtypeStruct((rows, 1), F32),
        ),
        compiler_params=pltpu.CompilerParams(vmem_limit_bytes=24 * 2**20),
        name="join_last",
    )(hidden, grad_norm, grad, down_t)


def adam_update(params_old, first_old, second_old, slot_grad, live):
    first_step = BETA_FIRST * first_old + (1.0 - BETA_FIRST) * slot_grad
    second_step = BETA_SECOND * second_old + (1.0 - BETA_SECOND) * slot_grad * slot_grad
    step_size = first_step / FIRST_FIX / (jnp.sqrt(second_step / SECOND_FIX) + ADAM_EPS)
    params_step = (params_old.astype(jnp.float32) - LEARN_RATE * step_size).astype(jnp.bfloat16)
    return (
        jnp.where(live, params_step, params_old),
        jnp.where(live, first_step, first_old),
        jnp.where(live, second_step, second_old),
    )


def on_device(
    tokens,
    cotangent,
    gains,
    value_projection_weight,
    output_projection_weight,
    block_adapter_ids,
    job_adapter,
    job_slab,
    token_counts,
    slot_adapter_params,
    first_moment,
    second_moment,
):
    section_index = lax.axis_index("section")
    owner_index = lax.axis_index("dp")
    section_total = lax.axis_size("section")
    owner_total = lax.axis_size("dp")
    tok_dev, hidden_width = tokens.shape
    value_feature_width = value_projection_weight.shape[2]
    panel_width = slot_adapter_params.shape[2]
    slab_count = owner_total // 2
    block_total = block_adapter_ids.shape[0]
    local_blocks = block_total // owner_total
    block_rows = tok_dev // local_blocks
    adapter_total = token_counts.shape[0]
    divide_position = hidden_width * ADAPTER_RANK
    gain_row = gains[0]
    shard_rows = value_projection_weight.shape[1]
    my_gain = lax.dynamic_slice_in_dim(gain_row, owner_index * shard_rows, shard_rows)
    scaled_value = (value_projection_weight[0].astype(F32) * my_gain[:, None]).astype(BF16)
    value_full = lax.all_gather(scaled_value, "dp", axis=0, tiled=True)
    output_full = lax.all_gather(output_projection_weight[0], "dp", axis=0, tiled=True)
    my_jobs = lax.dynamic_index_in_dim(job_adapter, owner_index, 0, keepdims=False)
    my_blocks = lax.dynamic_slice_in_dim(
        block_adapter_ids, owner_index * local_blocks, local_blocks
    )
    slab_ids = jnp.arange(slab_count, dtype=jnp.int32)
    matching = (job_adapter[None, None] == my_blocks[:, None, None, None]) & (
        job_slab[None, None] == slab_ids[None, :, None, None]
    )
    owner_ids = jnp.arange(owner_total, dtype=jnp.int32)
    source_owner = jnp.sum(jnp.where(matching, owner_ids[None, None, :, None], 0), axis=(2, 3))
    own_select = (block_adapter_ids[:, None] == my_jobs[None, :]) & (my_jobs[None, :] >= 0)
    slot_rows = jnp.arange(local_blocks, dtype=jnp.int32)[:, None]

    def hand_out(owned):
        picked = jnp.dot(own_select.astype(jnp.bfloat16), owned, preferred_element_type=jnp.float32)
        return picked.astype(jnp.bfloat16).reshape(owner_total, local_blocks, panel_width)

    def assemble(arrived):
        gathered_slabs = arrived[source_owner, slot_rows]
        return gathered_slabs.reshape(local_blocks, slab_count * panel_width)

    gathered_panels = assemble(
        lax.all_to_all(
            hand_out(slot_adapter_params[0]), "dp", split_axis=0, concat_axis=0, tiled=True
        )
    )
    down_t = (
        gathered_panels[0, :divide_position].reshape(hidden_width, ADAPTER_RANK).T.astype(F32)
        * gain_row[None, :]
    ).astype(BF16)
    up = gathered_panels[0, divide_position:].reshape(ADAPTER_RANK, value_feature_width)
    rows = tok_dev // MICRO
    last = section_total - 1
    token_micro = [tokens[m * rows : (m + 1) * rows] for m in range(MICRO)]
    cot_micro = [cotangent[m * rows : (m + 1) * rows] for m in range(MICRO)]
    ahead_pairs = [(i, i + 1) for i in range(last)]
    back_pairs = [(i + 1, i) for i in range(last)]
    wide_zero = lambda: jnp.zeros((rows, hidden_width), BF16)

    def prepare_last(_):
        gv, gl = reverse_first(cotangent, output_full, up)
        return gv, gl, spread(gv, gl, value_full, down_t)

    def prepare_none(_):
        return (
            jnp.zeros((tok_dev, value_feature_width), BF16),
            jnp.zeros((tok_dev, ADAPTER_RANK), BF16),
            jnp.zeros((tok_dev, hidden_width), F32),
        )

    last_gv, last_gl, last_norm = lax.cond(section_index == last, prepare_last, prepare_none, None)

    entering, ahead_state, ahead_sent = {}, {}, {}
    back_state, back_sent, last_state = {}, {}, {}
    for step in range(2 * last * LAG + MICRO):
        active = [s for s in range(last) if 0 <= step - LAG * s < MICRO]
        if step - LAG in ahead_sent:
            entering[step] = ahead_sent[step - LAG]
        if active:
            if step < MICRO:
                entering[step] = (
                    jnp.where(section_index == 0, token_micro[step], entering[step])
                    if step in entering
                    else token_micro[step]
                )
            is_active = (section_index >= active[0]) & (section_index <= active[-1])
            shape_of = jax.eval_shape(ahead, entering[step], down_t, up, value_full, output_full)
            result = lax.cond(
                is_active,
                lambda h: tuple(ahead(h, down_t, up, value_full, output_full)),
                lambda h: tuple(jnp.zeros(x.shape, x.dtype) for x in shape_of),
                entering[step],
            )
            ahead_state[step] = result[1:]
            ahead_sent[step] = lax.ppermute(result[0], "section", ahead_pairs)
        m_last = step - LAG * last
        branch = {}
        if 0 <= m_last < MICRO:
            branch[last] = m_last
        for s in range(last):
            m = step - LAG * (2 * last - s)
            if 0 <= m < MICRO:
                branch[s] = m
        if branch:
            incoming = back_sent.get(step - LAG)

            def nothing(_):
                return (
                    wide_zero(),
                    jnp.zeros((rows, value_feature_width), BF16),
                    jnp.zeros((rows, ADAPTER_RANK), BF16),
                    jnp.zeros((rows, ADAPTER_RANK), F32),
                    jnp.zeros((rows, 1), F32),
                )

            def make(s, m):
                def run_last(_):
                    prev, low, scale = join_last(
                        entering[step],
                        last_norm[m * rows : (m + 1) * rows],
                        cot_micro[m],
                        down_t,
                    )
                    return (prev,) + nothing(None)[1:3] + (low, scale)

                def run_first(_):
                    gv, gl = reverse_first(incoming, output_full, up)
                    return (wide_zero(), gv, gl) + nothing(None)[3:]

                def run_middle(_):
                    before = LAG * s + m
                    u, low, scale = ahead_state[before]
                    prev, gv, gl = reverse(
                        incoming, output_full, value_full, down_t, up, entering[before], u, low, scale
                    )
                    return (prev, gv, gl) + nothing(None)[3:]

                return run_last if s == last else run_first if s == 0 else run_middle

            result = lax.switch(
                section_index,
                [make(s, branch[s]) if s in branch else nothing for s in range(section_total)],
                None,
            )
            back_state[step] = result[1:3]
            last_state[step] = result[3:]
            if any(s > 0 for s in branch):
                back_sent[step] = lax.ppermute(result[0], "section", back_pairs)

    def gradients(s):
        def run(_):
            if s == last:
                steps = [LAG * last + m for m in range(MICRO)]
                gv, gl = last_gv, last_gl
                low = jnp.concatenate([last_state[k][0] for k in steps])
                scale = jnp.concatenate([last_state[k][1] for k in steps])
            else:
                steps = [LAG * s + m for m in range(MICRO)]
                later = [LAG * (2 * last - s) + m for m in range(MICRO)]
                gv = jnp.concatenate([back_state[k][0] for k in later])
                gl = jnp.concatenate([back_state[k][1] for k in later])
                low = jnp.concatenate([ahead_state[k][1] for k in steps])
                scale = jnp.concatenate([ahead_state[k][2] for k in steps])
            hidden = jnp.concatenate([entering[k] for k in steps]) if s else tokens
            scaled = (scale * gl.astype(F32)).astype(BF16)
            down_grad = contract_leading(hidden, scaled) * gain_row[:, None]
            low_rows = (scale * low).astype(BF16)
            up_grad = ADAPTER_SCALE * contract_leading(low_rows, gv)
            return jnp.concatenate(
                [down_grad.astype(BF16).reshape(-1), up_grad.astype(BF16).reshape(-1)]
            )

        return run

    block_grads = lax.switch(section_index, [gradients(s) for s in range(section_total)], None)
    outgoing = (
        jnp.zeros((owner_total, local_blocks, panel_width), BF16)
        .at[source_owner, slot_rows]
        .set(block_grads.reshape(local_blocks, slab_count, panel_width))
    )
    arrived = lax.all_to_all(outgoing, "dp", split_axis=0, concat_axis=0, tiled=True)
    summed = jnp.dot(
        own_select.astype(BF16).T,
        arrived.reshape(block_total, panel_width),
        preferred_element_type=F32,
    )
    live = my_jobs >= 0
    adapter_ids = jnp.arange(adapter_total, dtype=jnp.int32)
    slot_counts = jnp.sum(
        jnp.where(adapter_ids[None, :] == my_jobs[:, None], token_counts[None, :], 0), axis=1
    )
    slot_counts = jnp.where(live, slot_counts, 1)
    slot_grad = summed / slot_counts.astype(jnp.float32)[:, None]
    params_new, first_new, second_new = adam_update(
        slot_adapter_params[0], first_moment[0], second_moment[0], slot_grad, live[:, None]
    )
    returned = assemble(
        lax.all_to_all(hand_out(params_new), "dp", split_axis=0, concat_axis=0, tiled=True)
    )
    return (params_new[None], first_new[None], second_new[None], returned[None])


def solution(mesh):
    return jax.shard_map(
        on_device,
        mesh=mesh,
        in_specs=(
            P("dp", None),
            P("dp", None),
            P("section", None),
            P("section", "dp", None),
            P("section", "dp", None),
            P(),
            P(),
            P(),
            P(),
            P("section", "dp", None),
            P("section", "dp", None),
            P("section", "dp", None),
        ),
        out_specs=(
            P("section", "dp", None),
            P("section", "dp", None),
            P("section", "dp", None),
            P("section", "dp", None),
        ),
        check_vma=False,
    )
```

time: 1020 us -> 630 us (0.62)
  matrix products: 352 us -> 10 us
  Pallas kernels: 0 us -> 123 us
  other arithmetic: 107 us -> 22.5 us
  local copies, waits for them, and re-layouts: 89.5 us -> 53.8 us
  starting transfers between devices: 133 us -> 100 us
  loops' own time: 16.6 us -> 3.6 us
    dot_general x57 -> x1, matrix products: 318 us -> 6.28 us  [on_device(): jnp.dot(own_select.astype(BF16).T, arrived.reshape(block_total, panel_wid...]
    pallas_call x0 -> x8, Pallas kernels: none -> 123 us  [the longest x4 83.8 us: ahead(): pl.pallas_call(ahead_kernel, grid=(2 * chunks,), in_specs=[pl.BlockSpec((...]
    scatter-add x11 -> x0, other arithmetic: 33.9 us -> none  [backward_step(): block_grads.at[block_slot_index].add(jnp.where(is_valid, grad_term, 0.0))]
    dynamic_update_slice x44 -> x0, other arithmetic: 33.6 us -> none  [put_slot(): lax.dynamic_update_index_in_dim(saved_array, jnp.where(is_valid, new_valu...]
    dynamic_slice x55 -> x1, local copies, waits for them, and re-layouts: 34.2 us -> 0.77 us  [on_device(): lax.dynamic_slice_in_dim(gain_row, owner_index * shard_rows, shard_rows)]
    concatenate x15 -> x1, local copies, waits for them, and re-layouts: 30.3 us -> 0.01 us  [on_device(): outgoing = jnp.zeros((owner_total, local_blocks, panel_width), BF16).at[s...]
    dot_general x16 -> x2, matrix products: 31.7 us -> 2.3 us  [contract_leading(): lax.dot_general(left, right, (((0,), (0,)), ((), ())), preferred_element_...]
    another operation x19 -> x60, local copies, waits for them, and re-layouts: 5.06 us -> 27.2 us
  transfers between devices with their start and end apart: 27 -> 21, of which waited for: 27 -> 16; matrix products, arithmetic and copies ran while one was open for 9% -> 8% of each run, Pallas kernels for 0% -> 8%
where the time goes in v1:
time: 630 us; the launch traced here: 618 us
  waiting for transfers between devices  289 us (46%)
  Pallas kernels  123 us (20%)
  starting transfers between devices  100 us (16%)
  local copies, waits for them, and re-layouts  53.8 us (9%)
  other arithmetic  22.5 us (4%)
  between operations  14.8 us (2%)
  matrix products  10 us (2%)
    ppermute x8, waiting for transfers between devices, on_device(): back_sent[step] = lax.ppermute(result[0], 'section', back_pairs)  123 us
    pallas_call x4, Pallas kernels, ahead(): pl.pallas_call(ahead_kernel, grid=(2 * chunks,), in_specs=[pl.BlockSpec((...  83.8 us
    all_gather x1, waiting for transfers between devices, on_device(): lax.all_gather(output_projection_weight[0], 'dp', axis=0, tiled=True)  74.4 us
    ppermute x8, starting transfers between devices, on_device(): ahead_sent[step] = lax.ppermute(result[0], 'section', ahead_pairs)  67.8 us
    pallas_call x4, Pallas kernels, reverse_first(): pl.pallas_call(first_kernel, grid=(width // CHUNK,), in_specs=[pl.BlockSp...  39.5 us
    all_gather x1, waiting for transfers between devices, on_device(): value_full = lax.all_gather(scaled_value, 'dp', axis=0, tiled=True)  36.5 us
    another operation x59, local copies, waits for them, and re-layouts  27.2 us
    ppermute x8, waiting for transfers between devices, on_device(): ahead_sent[step] = lax.ppermute(result[0], 'section', ahead_pairs)  20.8 us
  transfers between devices with their start and end apart: 21, of which 16 were waited for; matrix products, arithmetic and copies ran while one was open for 8% of the time, Pallas kernels for 8%

profile of v1, /device:TPU:1, one launch (start us, length us, event | category | flops | bytes accessed | tf_op | source)
XLA Modules:
  0.0 617.8 jit_solution(10540356240086839988)
XLA Ops:
  29.0 15.2 %all-to-all-done = bf16[32,2,4608]{2,1,0:T(2,128)(2,1)S(1)} async-done(((bf16[32,2,4608]{2,1,0:T(2,128)(2,1)}), bf16[32,2,4608]{2,1,0:T(2,128)(2,1)S(1)}, u32[]{:S(2)}, u32[]{:S(2)}) %all-to-all-start) | async-done | bytes 589856 | tf_op jit(solution)/shard_map/all_to_all | solution.py:345
  55.1 36.5 %all-gather.4.cloned.1.call-done = bf16[8192,1024]{1,0:T(8,128)(2,1)} async-done(((bf16[256,1024]{1,0:T(8,128)(2,1)}), bf16[8192,1024]{1,0:T(8,128)(2,1)}) %all-gather.4.cloned.1.call-update) | async-done | bytes 16777232 | tf_op jit(solution)/shard_map/all_gather | solution.py:321
  91.6 74.4 %all-gather.6.cloned.1.call-done = bf16[1,8192,1024]{2,1,0:T(8,128)(2,1)} async-done(((bf16[1,256,1024]{2,1,0:T(8,128)(2,1)}), bf16[1,8192,1024]{2,1,0:T(8,128)(2,1)}) %all-gather.6.cloned.1.call-update) | async-done | bytes 16777232 | tf_op jit(solution)/shard_map/all_gather | solution.py:322
  165.9 22.8 %conditional.20 = (bf16[32,8192]{1,0:T(8,128)(2,1)S(1)}, f32[32,16]{1,0:T(8,128)}, f32[32,1]{1,0:T(8,128)}) conditional(s32[]{:T(128)} %convert_element_type.127, () %tuple.240, (bf16[128,8192]{1,0:T(8,128)(2,1)}, bf16[16,8192]{0,1:T(8,128)(2,1)S(1)}, bf16[16,1024]{1,0:T(8,128)(2,1)S(1)}, bf16[8192,1024]{1,0:T(8,128)(2,1)}, ...), branch_computations={%region_3.4_spmd, %region_4.5_spmd} | conditional | bytes 1572888 | solution.py:390
  167.8 20.9 %ahead.8 = (bf16[32,8192]{1,0:T(8,128)(2,1)S(1)}, f32[32,1024]{1,0:T(8,128)}, f32[32,16]{1,0:T(8,128)}, f32[32,1]{1,0:T(8,128)}) custom-call(bf16[32,8192]{1,0:T(8,128)(2,1)S(1)} %slice.34.h_ref, bf16[16,8192]{1,0:T(8,128)(2,1)S(1)} %copy.286.down_ref, bf16[16,1024]{1,0:T(8,128)(2,1)S(1)} %get-tuple-element.461.up_ref, ...), custom_call_target="tpu_custom_call" | custom-call | tf_op jit(solution)/shard_map/cond/branch_1_fun/ahead/pallas_call | solution.py:81
  188.7 22.8 %conditional.21 = (bf16[32,8192]{1,0:T(8,128)(2,1)}, f32[32,16]{1,0:T(8,128)}, f32[32,1]{1,0:T(8,128)}) conditional(s32[]{:T(128)} %convert_element_type.127, () %tuple.242, (bf16[128,8192]{1,0:T(8,128)(2,1)}, bf16[16,8192]{0,1:T(8,128)(2,1)S(1)}, bf16[16,1024]{1,0:T(8,128)(2,1)S(1)}, bf16[8192,1024]{1,0:T(8,128)(2,1)}, ...), branch_computations={%region_27.28_spmd, %region_28.29_spmd} | conditional | bytes 1572888 | solution.py:390
  190.6 21.0 %ahead.12 = (bf16[32,8192]{1,0:T(8,128)(2,1)}, f32[32,1024]{1,0:T(8,128)}, f32[32,16]{1,0:T(8,128)}, f32[32,1]{1,0:T(8,128)}) custom-call(bf16[32,8192]{1,0:T(8,128)(2,1)S(1)} %slice.39.h_ref, bf16[16,8192]{1,0:T(8,128)(2,1)S(1)} %copy.287.down_ref, bf16[16,1024]{1,0:T(8,128)(2,1)S(1)} %get-tuple-element.539.up_ref, ...), custom_call_target="tpu_custom_call" | custom-call | tf_op jit(solution)/shard_map/cond/branch_1_fun/ahead/pallas_call | solution.py:81
  224.5 11.1 %collective-permute-done = bf16[32,8192]{1,0:T(8,128)(2,1)} collective-permute-done((bf16[32,8192]{1,0:T(8,128)(2,1)S(1)}, bf16[32,8192]{1,0:T(8,128)(2,1)}, u32[]{:S(2)}, u32[]{:S(2)}) %collective-permute-start) | collective-permute-done | bytes 524320 | tf_op jit(solution)/shard_map/ppermute | solution.py:397
  237.7 21.8 %conditional.22 = ((bf16[32,8192]{1,0:T(8,128)(2,1)}, f32[32,1024]{1,0:T(8,128)}, f32[32,16]{1,0:T(8,128)S(1)}, f32[32,1]{1,0:T(8,128)S(1)})) conditional(s32[]{:T(128)} %convert_element_type.136, () %tuple.243, (bf16[32,8192]{1,0:T(8,128)(2,1)}, bf16[16,8192]{0,1:T(8,128)(2,1)S(1)}, bf16[16,1024]{1,0:T(8,128)(2,1)S(1)}, ...), branch_computations={%region_5.6_spmd, %region_6.7_spmd} | conditional | bytes 657590 | solution.py:390
  238.5 21.0 %ahead.9 = (bf16[32,8192]{1,0:T(8,128)(2,1)}, f32[32,1024]{1,0:T(8,128)}, f32[32,16]{1,0:T(8,128)S(1)}, f32[32,1]{1,0:T(8,128)S(1)}) custom-call(bf16[32,8192]{1,0:T(8,128)(2,1)} %get-tuple-element.467.h_ref, bf16[16,8192]{1,0:T(8,128)(2,1)S(1)} %copy.288.down_ref, bf16[16,1024]{1,0:T(8,128)(2,1)S(1)} %get-tuple-element.469.up_ref, ...), custom_call_target="tpu_custom_call" | custom-call | tf_op jit(solution)/shard_map/cond/branch_1_fun/ahead/pallas_call | solution.py:81
  263.9 21.9 %conditional.23 = ((bf16[32,8192]{1,0:T(8,128)(2,1)}, f32[32,1024]{1,0:T(8,128)}, f32[32,16]{1,0:T(8,128)S(1)}, f32[32,1]{1,0:T(8,128)})) conditional(s32[]{:T(128)} %convert_element_type.136, () %tuple.245, (bf16[32,8192]{1,0:T(8,128)(2,1)S(1)}, bf16[16,8192]{0,1:T(8,128)(2,1)S(1)}, bf16[16,1024]{1,0:T(8,128)(2,1)S(1)}, ...), branch_computations={%region_29.30_spmd, %region_30.31_spmd} | conditional | bytes 657590 | solution.py:390
  264.8 20.9 %ahead.13 = (bf16[32,8192]{1,0:T(8,128)(2,1)}, f32[32,1024]{1,0:T(8,128)}, f32[32,16]{1,0:T(8,128)S(1)}, f32[32,1]{1,0:T(8,128)}) custom-call(bf16[32,8192]{1,0:T(8,128)(2,1)S(1)} %get-tuple-element.545.h_ref, bf16[16,8192]{1,0:T(8,128)(2,1)S(1)} %copy.289.down_ref, bf16[16,1024]{1,0:T(8,128)(2,1)S(1)} %get-tuple-element.547.up_ref, ...), custom_call_target="tpu_custom_call" | custom-call | tf_op jit(solution)/shard_map/cond/branch_1_fun/ahead/pallas_call | solution.py:81
  289.2 22.9 %collective-permute-start.3 = (bf16[32,8192]{1,0:T(8,128)(2,1)}, bf16[32,8192]{1,0:T(8,128)(2,1)}, u32[]{:S(2)}, u32[]{:S(2)}) collective-permute-start(bf16[32,8192]{1,0:T(8,128)(2,1)} %get-tuple-element.773), channel_id=1, source_target_pairs={{0,32},{32,64},{64,96},{1,33},{33,65},{65,97},{2,34},{34,66},{66,9... | collective-permute-start | bytes 1572872 | tf_op jit(solution)/shard_map/ppermute | solution.py:397
  313.7 22.1 %collective-permute-start.9 = (bf16[32,8192]{1,0:T(8,128)(2,1)}, bf16[32,8192]{1,0:T(8,128)(2,1)}, u32[]{:S(2)}, u32[]{:S(2)}) collective-permute-start(bf16[32,8192]{1,0:T(8,128)(2,1)} %get-tuple-element.788), channel_id=1, source_target_pairs={{0,32},{32,64},{64,96},{1,33},{33,65},{65,97},{2,34},{34,66},{66,9... | collective-permute-start | bytes 1572872 | tf_op jit(solution)/shard_map/ppermute | solution.py:397
  350.4 11.0 %collective-permute-start.11 = (bf16[32,8192]{1,0:T(8,128)(2,1)}, bf16[32,8192]{1,0:T(8,128)(2,1)}, u32[]{:S(2)}, u32[]{:S(2)}) collective-permute-start(bf16[32,8192]{1,0:T(8,128)(2,1)} %get-tuple-element.793), channel_id=1, source_target_pairs={{0,32},{32,64},{64,96},{1,33},{33,65},{65,97},{2,34},{34,66},{66,9... | collective-permute-start | bytes 1572872 | tf_op jit(solution)/shard_map/ppermute | solution.py:397
  370.4 26.1 %collective-permute-done.10 = bf16[32,8192]{1,0:T(8,128)(2,1)} collective-permute-done((bf16[32,8192]{1,0:T(8,128)(2,1)}, bf16[32,8192]{1,0:T(8,128)(2,1)}, u32[]{:S(2)}, u32[]{:S(2)}) %collective-permute-start.10) | collective-permute-done | bytes 524320 | tf_op jit(solution)/shard_map/ppermute | solution.py:450
  421.5 36.7 %collective-permute-done.7 = bf16[32,8192]{1,0:T(8,128)(2,1)S(1)} collective-permute-done((bf16[32,8192]{1,0:T(8,128)(2,1)}, bf16[32,8192]{1,0:T(8,128)(2,1)S(1)}, u32[]{:S(2)}, u32[]{:S(2)}) %collective-permute-start.7) | collective-permute-done | bytes 524320 | tf_op jit(solution)/shard_map/ppermute | solution.py:450
  458.2 10.2 %conditional.30 = ((bf16[32,8192]{1,0:T(8,128)(2,1)S(1)}, bf16[32,1024]{1,0:T(8,128)(2,1)}, bf16[32,16]{1,0:T(8,128)(2,1)})) conditional(s32[]{:T(128)} %clamp.2, (bf16[32,8192]{1,0:T(8,128)(2,1)S(1)}, bf16[8192,1024]{1,0:T(8,128)(2,1)}, bf16[16,1024]{1,0:T(8,128)(2,1)S(1)}) %tuple.536, ...), branch_computations={%region_23.24_spmd, %region_24.25_spmd, %region_25.26_spmd, %regio... | conditional | bytes 590886 | solution.py:442
  470.5 12.7 %collective-permute-done.13 = bf16[32,8192]{1,0:T(8,128)(2,1)S(1)} collective-permute-done((bf16[32,8192]{1,0:T(8,128)(2,1)S(1)}, bf16[32,8192]{1,0:T(8,128)(2,1)S(1)}, u32[]{:S(2)}, u32[]{:S(2)}) %collective-permute-start.13) | collective-permute-done | bytes 524320 | tf_op jit(solution)/shard_map/ppermute | solution.py:450
  494.0 15.4 %collective-permute-done.14 = bf16[32,8192]{1,0:T(8,128)(2,1)S(1)} collective-permute-done((bf16[32,8192]{1,0:T(8,128)(2,1)}, bf16[32,8192]{1,0:T(8,128)(2,1)S(1)}, u32[]{:S(2)}, u32[]{:S(2)}) %collective-permute-start.14) | collective-permute-done | bytes 524320 | tf_op jit(solution)/shard_map/ppermute | solution.py:450
  519.0 14.2 %collective-permute-done.15 = bf16[32,8192]{1,0:T(8,128)(2,1)S(1)} collective-permute-done((bf16[32,8192]{1,0:T(8,128)(2,1)S(1)}, bf16[32,8192]{1,0:T(8,128)(2,1)S(1)}, u32[]{:S(2)}, u32[]{:S(2)}) %collective-permute-start.15) | collective-permute-done | bytes 524320 | tf_op jit(solution)/shard_map/ppermute | solution.py:450
  534.0 10.4 %conditional.38 = ((bf16[32,1024]{1,0:T(8,128)(2,1)}, bf16[32,16]{1,0:T(8,128)(2,1)S(1)})) conditional(s32[]{:T(128)} %clamp.2, (bf16[32,8192]{1,0:T(8,128)(2,1)}, bf16[8192,1024]{1,0:T(8,128)(2,1)}, bf16[16,1024]{1,0:T(8,128)(2,1)S(1)}) %tuple.557, () %tuple.294, () %tuple.295, () %tuple.296), branch_computations={%region_55.56_spmd, %region_56.57_spmd, %region_57.58_spmd, %regio... | conditional | bytes 66588 | solution.py:442
  534.0 10.4 %reverse_first.9 = (bf16[32,1024]{1,0:T(8,128)(2,1)}, bf16[32,16]{1,0:T(8,128)(2,1)S(1)}) custom-call(bf16[32,8192]{1,0:T(8,128)(2,1)} %get-tuple-element.618.grad_ref, bf16[8192,1024]{1,0:T(8,128)(2,1)} %get-tuple-element.619.output_ref, bf16[16,1024]{1,0:T(8,128)(2,1)S(1)} %get-tuple-element.620.up_ref), custom_call_target="tpu_custom_call" | custom-call | tf_op jit(solution)/shard_map/cond/branch_0_fun/reverse_first/pallas_call | solution.py:207
  568.5 11.4 %all-to-all-done.1 = bf16[32,2,4608]{2,1,0:T(2,128)(2,1)S(1)} async-done(((bf16[32,2,4608]{2,1,0:T(2,128)(2,1)}), bf16[32,2,4608]{2,1,0:T(2,128)(2,1)S(1)}, u32[]{:S(2)}, u32[]{:S(2)}) %all-to-all-start.1) | async-done | bytes 589856 | tf_op jit(solution)/shard_map/all_to_all | solution.py:483
  (222 shorter events, 246.6 us)
Async XLA Ops:
  7.2 84.4 %all-gather.4.cloned.1.call-start = ((), (), s32[]{:S(2)}) async-start(), calls=%async_computation.3 | async-start | bytes 17301504 | tf_op jit(solution)/shard_map/all_gather | solution.py:321
  10.0 155.9 %all-gather.6.cloned.1.call-start = ((), (), s32[]{:S(2)}) async-start(), calls=%async_computation.4 | async-start | bytes 17301504 | tf_op jit(solution)/shard_map/all_gather | solution.py:322
  17.2 27.1 %all-to-all-start = ((bf16[32,2,4608]{2,1,0:T(2,128)(2,1)}), bf16[32,2,4608]{2,1,0:T(2,128)(2,1)S(1)}, u32[]{:S(2)}, u32[]{:S(2)}) async-start(bf16[32,2,4608]{2,1,0:T(2,128)(2,1)} %reshape.182), calls=%async_computation | async-start | bytes 1179648 | tf_op jit(solution)/shard_map/all_to_all | solution.py:345
  55.0 289.3 %copy-start = (bf16[16,8192]{0,1:T(8,128)(2,1)}, bf16[16,8192]{0,1:T(8,128)(2,1)S(1)}, u32[]{:S(2)}) copy-start(bf16[16,8192]{0,1:T(8,128)(2,1)S(1)} %fusion.109) | copy-start | bytes 786436
  211.6 12.9 %collective-permute-start.1 = (bf16[32,8192]{1,0:T(8,128)(2,1)}, bf16[32,8192]{1,0:T(8,128)(2,1)S(1)}, u32[]{:S(2)}, u32[]{:S(2)}) collective-permute-start(bf16[32,8192]{1,0:T(8,128)(2,1)} %get-tuple-element.769), channel_id=1, source_target_pairs={{0,32},{32,64},{64,96},{1,33},{33,65},{65,97},{2,34},{34,66},{66,9... | collective-permute-start | bytes 1572872 | tf_op jit(solution)/shard_map/ppermute | solution.py:397
  212.9 22.7 %collective-permute-start = (bf16[32,8192]{1,0:T(8,128)(2,1)S(1)}, bf16[32,8192]{1,0:T(8,128)(2,1)}, u32[]{:S(2)}, u32[]{:S(2)}) collective-permute-start(bf16[32,8192]{1,0:T(8,128)(2,1)S(1)} %get-tuple-element.767), channel_id=1, source_target_pairs={{0,32},{32,64},{64,96},{1,33},{33,65},{65,97},{2,34},{34,66},{66,9... | collective-permute-start | bytes 1572872 | tf_op jit(solution)/shard_map/ppermute | solution.py:397
  259.5 28.2 %collective-permute-start.2 = (bf16[32,8192]{1,0:T(8,128)(2,1)}, bf16[32,8192]{1,0:T(8,128)(2,1)S(1)}, u32[]{:S(2)}, u32[]{:S(2)}) collective-permute-start(bf16[32,8192]{1,0:T(8,128)(2,1)} %get-tuple-element.772), channel_id=1, source_target_pairs={{0,32},{32,64},{64,96},{1,33},{33,65},{65,97},{2,34},{34,66},{66,9... | collective-permute-start | bytes 1572872 | tf_op jit(solution)/shard_map/ppermute | solution.py:397
  285.8 26.3 %collective-permute-start.8 = (bf16[32,8192]{1,0:T(8,128)(2,1)}, bf16[32,8192]{1,0:T(8,128)(2,1)S(1)}, u32[]{:S(2)}, u32[]{:S(2)}) collective-permute-start(bf16[32,8192]{1,0:T(8,128)(2,1)} %get-tuple-element.787), channel_id=1, source_target_pairs={{0,32},{32,64},{64,96},{1,33},{33,65},{65,97},{2,34},{34,66},{66,9... | collective-permute-start | bytes 1572872 | tf_op jit(solution)/shard_map/ppermute | solution.py:397
  289.2 50.3 %collective-permute-start.3 = (bf16[32,8192]{1,0:T(8,128)(2,1)}, bf16[32,8192]{1,0:T(8,128)(2,1)}, u32[]{:S(2)}, u32[]{:S(2)}) collective-permute-start(bf16[32,8192]{1,0:T(8,128)(2,1)} %get-tuple-element.773), channel_id=1, source_target_pairs={{0,32},{32,64},{64,96},{1,33},{33,65},{65,97},{2,34},{34,66},{66,9... | collective-permute-start | bytes 1572872 | tf_op jit(solution)/shard_map/ppermute | solution.py:397
  313.7 34.0 %collective-permute-start.9 = (bf16[32,8192]{1,0:T(8,128)(2,1)}, bf16[32,8192]{1,0:T(8,128)(2,1)}, u32[]{:S(2)}, u32[]{:S(2)}) collective-permute-start(bf16[32,8192]{1,0:T(8,128)(2,1)} %get-tuple-element.788), channel_id=1, source_target_pairs={{0,32},{32,64},{64,96},{1,33},{33,65},{65,97},{2,34},{34,66},{66,9... | collective-permute-start | bytes 1572872 | tf_op jit(solution)/shard_map/ppermute | solution.py:397
  342.2 22.5 %collective-permute-start.5 = (bf16[32,8192]{1,0:T(8,128)(2,1)}, bf16[32,8192]{1,0:T(8,128)(2,1)}, u32[]{:S(2)}, u32[]{:S(2)}) collective-permute-start(bf16[32,8192]{1,0:T(8,128)(2,1)} %get-tuple-element.778), channel_id=1, source_target_pairs={{0,32},{32,64},{64,96},{1,33},{33,65},{65,97},{2,34},{34,66},{66,9... | collective-permute-start | bytes 1572872 | tf_op jit(solution)/shard_map/ppermute | solution.py:397
  346.3 20.4 %collective-permute-start.4 = (bf16[32,8192]{1,0:T(8,128)(2,1)}, bf16[32,8192]{1,0:T(8,128)(2,1)S(1)}, u32[]{:S(2)}, u32[]{:S(2)}) collective-permute-start(bf16[32,8192]{1,0:T(8,128)(2,1)} %get-tuple-element.774), channel_id=1, source_target_pairs={{32,0},{64,32},{96,64},{33,1},{65,33},{97,65},{34,2},{66,34},{98,6... | collective-permute-start | bytes 1572872 | tf_op jit(solution)/shard_map/ppermute | solution.py:450
  350.4 20.1 %collective-permute-start.11 = (bf16[32,8192]{1,0:T(8,128)(2,1)}, bf16[32,8192]{1,0:T(8,128)(2,1)}, u32[]{:S(2)}, u32[]{:S(2)}) collective-permute-start(bf16[32,8192]{1,0:T(8,128)(2,1)} %get-tuple-element.793), channel_id=1, source_target_pairs={{0,32},{32,64},{64,96},{1,33},{33,65},{65,97},{2,34},{34,66},{66,9... | collective-permute-start | bytes 1572872 | tf_op jit(solution)/shard_map/ppermute | solution.py:397
  363.4 33.2 %collective-permute-start.10 = (bf16[32,8192]{1,0:T(8,128)(2,1)}, bf16[32,8192]{1,0:T(8,128)(2,1)}, u32[]{:S(2)}, u32[]{:S(2)}) collective-permute-start(bf16[32,8192]{1,0:T(8,128)(2,1)} %get-tuple-element.789), channel_id=1, source_target_pairs={{32,0},{64,32},{96,64},{33,1},{65,33},{97,65},{34,2},{66,34},{98,6... | collective-permute-start | bytes 1572872 | tf_op jit(solution)/shard_map/ppermute | solution.py:450
  368.9 27.6 %copy-start.27 = (bf16[32,16]{1,0:T(8,128)(2,1)}, bf16[32,16]{1,0:T(8,128)(2,1)S(1)}, u32[]{:S(2)}) copy-start(bf16[32,16]{1,0:T(8,128)(2,1)S(1)} %get-tuple-element.816) | copy-start | bytes 3076
  369.0 27.6 %copy-start.20 = (bf16[32,1024]{1,0:T(8,128)(2,1)}, bf16[32,1024]{1,0:T(8,128)(2,1)S(1)}, u32[]{:S(2)}) copy-start(bf16[32,1024]{1,0:T(8,128)(2,1)S(1)} %get-tuple-element.818) | copy-start | bytes 196612
  369.0 38.7 %collective-permute-start.6 = (bf16[32,8192]{1,0:T(8,128)(2,1)}, bf16[32,8192]{1,0:T(8,128)(2,1)S(1)}, u32[]{:S(2)}, u32[]{:S(2)}) collective-permute-start(bf16[32,8192]{1,0:T(8,128)(2,1)} %get-tuple-element.779), channel_id=1, source_target_pairs={{32,0},{64,32},{96,64},{33,1},{65,33},{97,65},{34,2},{66,34},{98,6... | collective-permute-start | bytes 1572872 | tf_op jit(solution)/shard_map/ppermute | solution.py:450
  398.6 20.3 %collective-permute-start.12 = (bf16[32,8192]{1,0:T(8,128)(2,1)}, bf16[32,8192]{1,0:T(8,128)(2,1)S(1)}, u32[]{:S(2)}, u32[]{:S(2)}) collective-permute-start(bf16[32,8192]{1,0:T(8,128)(2,1)} %get-tuple-element.794), channel_id=1, source_target_pairs={{32,0},{64,32},{96,64},{33,1},{65,33},{97,65},{34,2},{66,34},{98,6... | collective-permute-start | bytes 1572872 | tf_op jit(solution)/shard_map/ppermute | solution.py:450
  409.2 49.0 %collective-permute-start.7 = (bf16[32,8192]{1,0:T(8,128)(2,1)}, bf16[32,8192]{1,0:T(8,128)(2,1)S(1)}, u32[]{:S(2)}, u32[]{:S(2)}) collective-permute-start(bf16[32,8192]{1,0:T(8,128)(2,1)} %get-tuple-element.785), channel_id=1, source_target_pairs={{32,0},{64,32},{96,64},{33,1},{65,33},{97,65},{34,2},{66,34},{98,6... | collective-permute-start | bytes 1572872 | tf_op jit(solution)/shard_map/ppermute | solution.py:450
  420.2 62.9 %collective-permute-start.13 = (bf16[32,8192]{1,0:T(8,128)(2,1)S(1)}, bf16[32,8192]{1,0:T(8,128)(2,1)S(1)}, u32[]{:S(2)}, u32[]{:S(2)}) collective-permute-start(bf16[32,8192]{1,0:T(8,128)(2,1)S(1)} %get-tuple-element.800), channel_id=1, source_target_pairs={{32,0},{64,32},{96,64},{33,1},{65,33},{97,65},{34,2},{66,34},{98,6... | collective-permute-start | bytes 1572872 | tf_op jit(solution)/shard_map/ppermute | solution.py:450
  469.2 40.3 %collective-permute-start.14 = (bf16[32,8192]{1,0:T(8,128)(2,1)}, bf16[32,8192]{1,0:T(8,128)(2,1)S(1)}, u32[]{:S(2)}, u32[]{:S(2)}) collective-permute-start(bf16[32,8192]{1,0:T(8,128)(2,1)} %copy-done.14), channel_id=1, source_target_pairs={{32,0},{64,32},{96,64},{33,1},{65,33},{97,65},{34,2},{66,34},{98,6... | collective-permute-start | bytes 1572872 | tf_op jit(solution)/shard_map/ppermute | solution.py:450
  492.7 40.5 %collective-permute-start.15 = (bf16[32,8192]{1,0:T(8,128)(2,1)S(1)}, bf16[32,8192]{1,0:T(8,128)(2,1)S(1)}, u32[]{:S(2)}, u32[]{:S(2)}) collective-permute-start(bf16[32,8192]{1,0:T(8,128)(2,1)S(1)} %get-tuple-element.804), channel_id=1, source_target_pairs={{32,0},{64,32},{96,64},{33,1},{65,33},{97,65},{34,2},{66,34},{98,6... | collective-permute-start | bytes 1572872 | tf_op jit(solution)/shard_map/ppermute | solution.py:450
  558.7 21.2 %all-to-all-start.1 = ((bf16[32,2,4608]{2,1,0:T(2,128)(2,1)}), bf16[32,2,4608]{2,1,0:T(2,128)(2,1)S(1)}, u32[]{:S(2)}, u32[]{:S(2)}) async-start(bf16[32,2,4608]{2,1,0:T(2,128)(2,1)} %reshape.184), calls=%async_computation.1 | async-start | bytes 1179648 | tf_op jit(solution)/shard_map/all_to_all | solution.py:483
  591.7 15.9 %all-to-all-start.2 = ((bf16[32,2,4608]{2,1,0:T(2,128)(2,1)}), bf16[32,2,4608]{2,1,0:T(2,128)(2,1)S(1)}, u32[]{:S(2)}, u32[]{:S(2)}) async-start(bf16[32,2,4608]{2,1,0:T(2,128)(2,1)} %reshape.186), calls=%async_computation.2 | async-start | bytes 1179648 | tf_op jit(solution)/shard_map/all_to_all | solution.py:500
  (30 other events, 311.5 us)
Sparse Core Ops, SparseCore 0:
  10.8 80.7 all-gather.3
  93.8 72.0 all-gather.5
